TPU v7x, 128 devices: a whole 4x4x4 slice. The times are simulated.
128 devices in a mesh: dp: 16 (over y, x), mp: 8 (over z, core).
Axes of the slice: x: 4, y: 4, z: 4, core: 2. Of those that a mesh axis runs over, the one named last changes fastest.
Arguments:
- tokens: bfloat16 [8192, 4096], P('dp'), may hold values from -6 to 6
- cache: bfloat16 [384, 128, 896], P('dp'), may hold values from -220 to 220
- nb_row: int32 [128, 2], P('dp'), may hold values from 0 to 23
- nb_owner: int32 [128, 2], P('dp'), may hold values from 0 to 15, all different within a row; in each aligned block of 8 rows (0 to 7, 8 to 15, ...) at most 3 rows name the same one
- nb_len: int32 [128, 2], P('dp'), may hold values from 32 to 128, as said below
- w_query: bfloat16 [4096, 4096], P('dp', 'mp'), may hold values from -0.09375 to 0.09375
- w_key: bfloat16 [896, 4096], P('dp', 'mp'), may hold values from -0.1875 to 0.1875
- w_value: bfloat16 [896, 4096], P('dp', 'mp'), may hold values from -0.1875 to 0.1875
- w_out: bfloat16 [4096, 4096], P('mp', 'dp'), may hold values from -0.09375 to 0.09375
- grad_out: bfloat16 [8192, 4096], P('dp'), may hold values from -6 to 6
Outputs:
- mixed: bfloat16 [8192, 4096], P('dp', 'mp')
- grad_tokens: bfloat16 [8192, 4096], P('dp', 'mp')
- grad_query: float32 [4096, 4096], P('dp', 'mp')
- grad_key: float32 [896, 4096], P('dp', 'mp')
- grad_value: float32 [896, 4096], P('dp', 'mp')
- grad_wout: float32 [4096, 4096], P('mp', 'dp')
Inputs may be any that keep to these rules, and one draw needn't show every extreme that they name: `nb_owner`: among the 8 stretches of one index of dp no shard is named more than 3 times, a bound that some block reaches; the 2 neighbours of a stretch lie on different shards. `nb_len`: the first neighbour of every stretch has all 128 tokens.
All inputs are finite; a program needn't handle non-finite values.
Results may differ from a plain program's by a relative error of at most 0.014.
The roundings to bfloat16 on the way count: a program that leaves them out, or rounds other values in their place, can miss the bound.
Values may be sent and summed in bfloat16 or wider, within the bound.
No kernel may reach another device: no remote copies, remote signals or barrier semaphores. Data moves between devices by JAX's collectives and lax.ppermute only.
A program may use at most 128 MiB of HBM per device.

v0:
```python
import jax
import jax.numpy as jnp
from jax import lax
from jax.sharding import PartitionSpec as P

HD = 128
CL = 64
KN = 2
CAP = 3


def on_device(tokens, cache, nb_row, nb_owner, nb_len, w_query, w_key, w_value, w_out, grad_out):
    dp_count = lax.axis_size("dp")
    mp_count = lax.axis_size("mp")
    mp_place = lax.axis_index("mp")
    tok_rows, width = tokens.shape
    head_span = w_query.shape[1]
    heads_here = head_span // HD
    stretch_count = nb_row.shape[0]
    request_count = stretch_count * KN
    cache_rows, block_len, enc_width = cache.shape
    width_share = width // mp_count
    score_scale = HD ** (-0.5)
    wide_tokens = tokens.astype(jnp.float32)
    inv_rms = lax.rsqrt(jnp.mean(wide_tokens * wide_tokens, axis=1, keepdims=True) + 1e-06)
    normed_wide = wide_tokens * inv_rms
    normed = normed_wide.astype(jnp.bfloat16)
    query_full = lax.all_gather(w_query, "dp", axis=0, tiled=True)
    output_full = lax.all_gather(w_out, "dp", axis=1, tiled=True)
    queries = jnp.dot(normed, query_full, preferred_element_type=jnp.float32).astype(jnp.bfloat16)
    owners = nb_owner.reshape(-1)
    wanted = nb_row.reshape(-1)
    req_order = jnp.arange(request_count)
    earlier = (owners[:, None] == owners[None, :]) & (req_order[None, :] < req_order[:, None])
    rank_seen = jnp.sum(earlier.astype(jnp.int32), axis=1)
    slot_of = owners * CAP + rank_seen
    slot_hits = (slot_of[:, None] == jnp.arange(dp_count * CAP)[None, :]).astype(jnp.int32)
    asked_ids = (jnp.sum(slot_hits * (wanted[:, None] + 1), axis=0) - 1).reshape(dp_count, CAP)
    picked_rows = jnp.clip(
        lax.all_to_all(asked_ids, "dp", split_axis=0, concat_axis=0, tiled=True), 0, cache_rows - 1
    )
    picked = jnp.take(cache, picked_rows, axis=0)
    arrived = lax.all_to_all(picked, "dp", split_axis=0, concat_axis=0, tiled=True)
    arrived = arrived.reshape(dp_count * CAP, arrived.shape[2], enc_width)
    blocks = jnp.take(arrived, slot_of, axis=0)
    flat_blocks = blocks.reshape(request_count * block_len, enc_width)
    key_sum = jnp.dot(
        flat_blocks,
        lax.all_gather(w_key, "dp", axis=0, tiled=True),
        preferred_element_type=jnp.float32,
    )
    value_sum = jnp.dot(
        flat_blocks,
        lax.all_gather(w_value, "dp", axis=0, tiled=True),
        preferred_element_type=jnp.float32,
    )
    keys = key_sum.astype(jnp.bfloat16).reshape(stretch_count, KN * block_len, heads_here, HD)
    values = value_sum.astype(jnp.bfloat16).reshape(stretch_count, KN * block_len, heads_here, HD)
    positions = jnp.arange(block_len)
    key_valid = (positions[None, None, :] < nb_len[:, :, None]).reshape(
        stretch_count, KN * block_len
    )
    query_blocks = queries.reshape(stretch_count, CL, heads_here, HD)
    scores = (
        jnp.einsum("cqhd,ckhd->chqk", query_blocks, keys, preferred_element_type=jnp.float32)
        * score_scale
    )
    scores = jnp.where(key_valid[:, None, None, :], scores, -1e30)
    row_top = jnp.max(scores, axis=3, keepdims=True)
    weights_exp = jnp.exp(scores - row_top)
    prob_wide = weights_exp / jnp.sum(weights_exp, axis=3, keepdims=True)
    prob = prob_wide.astype(jnp.bfloat16)
    attended = jnp.einsum(
        "chqk,ckhd->cqhd", prob, values, preferred_element_type=jnp.float32
    ).astype(jnp.bfloat16)
    attended = attended.reshape(tok_rows, head_span)
    partial_out = jnp.dot(attended, output_full, preferred_element_type=jnp.float32)
    summed_out = lax.psum_scatter(
        partial_out.astype(jnp.bfloat16), "mp", scatter_dimension=1, tiled=True
    ).astype(jnp.float32)
    token_cols = lax.dynamic_slice_in_dim(wide_tokens, mp_place * width_share, width_share, 1)
    mixed = (token_cols + summed_out).astype(jnp.bfloat16)
    grad_attn = jnp.einsum(
        "td,sd->ts", grad_out, output_full, preferred_element_type=jnp.float32
    ).astype(jnp.bfloat16)
    grad_wout_part = jnp.einsum("ts,td->sd", attended, grad_out, preferred_element_type=jnp.float32)
    grad_blocks = grad_attn.reshape(stretch_count, CL, heads_here, HD)
    grad_prob = jnp.einsum(
        "cqhd,ckhd->chqk", grad_blocks, values, preferred_element_type=jnp.float32
    )
    grad_values = jnp.einsum(
        "chqk,cqhd->ckhd", prob, grad_blocks, preferred_element_type=jnp.float32
    ).astype(jnp.bfloat16)
    delta_rows = jnp.sum(prob_wide * grad_prob, axis=3, keepdims=True)
    grad_scores = (prob_wide * (grad_prob - delta_rows) * score_scale).astype(jnp.bfloat16)
    grad_queries = jnp.einsum(
        "chqk,ckhd->cqhd", grad_scores, keys, preferred_element_type=jnp.float32
    ).astype(jnp.bfloat16)
    grad_queries = grad_queries.reshape(tok_rows, head_span)
    grad_keys = jnp.einsum(
        "chqk,cqhd->ckhd", grad_scores, query_blocks, preferred_element_type=jnp.float32
    ).astype(jnp.bfloat16)
    grad_keys = grad_keys.reshape(request_count * block_len, head_span)
    grad_values = grad_values.reshape(request_count * block_len, head_span)
    grad_wq_part = jnp.einsum("td,ts->ds", normed, grad_queries, preferred_element_type=jnp.float32)
    grad_wk_part = jnp.einsum(
        "re,rs->es", flat_blocks, grad_keys, preferred_element_type=jnp.float32
    )
    grad_wv_part = jnp.einsum(
        "re,rs->es", flat_blocks, grad_values, preferred_element_type=jnp.float32
    )
    grad_query, grad_key, grad_value, grad_wout = (
        lax.psum_scatter(
            grad_wq_part.astype(jnp.bfloat16), "dp", scatter_dimension=0, tiled=True
        ).astype(jnp.float32),
        lax.psum_scatter(
            grad_wk_part.astype(jnp.bfloat16), "dp", scatter_dimension=0, tiled=True
        ).astype(jnp.float32),
        lax.psum_scatter(
            grad_wv_part.astype(jnp.bfloat16), "dp", scatter_dimension=0, tiled=True
        ).astype(jnp.float32),
        lax.psum_scatter(
            grad_wout_part.astype(jnp.bfloat16), "dp", scatter_dimension=1, tiled=True
        ).astype(jnp.float32),
    )
    grad_normed_part = jnp.einsum(
        "ts,ds->td", grad_queries, query_full, preferred_element_type=jnp.float32
    )
    out_cols = lax.dynamic_slice_in_dim(grad_out, mp_place * width_share, width_share, 1).astype(
        jnp.float32
    )
    grad_normed = lax.psum(grad_normed_part.astype(jnp.bfloat16), "mp").astype(jnp.float32)
    stat_rows = jnp.mean(grad_normed * normed_wide, axis=1, keepdims=True)
    grad_full = inv_rms * (grad_normed - normed_wide * stat_rows)
    grad_here = lax.dynamic_slice_in_dim(grad_full, mp_place * width_share, width_share, 1)
    grad_tokens = (out_cols + grad_here).astype(jnp.bfloat16)
    return (mixed, grad_tokens, grad_query, grad_key, grad_value, grad_wout)


def solution(mesh):
    return jax.shard_map(
        on_device,
        mesh=mesh,
        in_specs=(
            P("dp", None),
            P("dp", None, None),
            P("dp", None),
            P("dp", None),
            P("dp", None),
            P("dp", "mp"),
            P("dp", "mp"),
            P("dp", "mp"),
            P("mp", "dp"),
            P("dp", None),
        ),
        out_specs=(
            P("dp", "mp"),
            P("dp", "mp"),
            P("dp", "mp"),
            P("dp", "mp"),
            P("dp", "mp"),
            P("mp", "dp"),
        ),
        check_vma=False,
    )
```

profile of v0, /device:TPU:0, one launch (start us, length us, event | category | flops | bytes accessed | tf_op | source)
XLA Modules:
  0.0 782.3 jit_solution(9086871764430105319)
XLA Ops:
  7.2 0.7 all-gather.3.cloned.1.call-update
  7.9 0.7 broadcast_add_fusion
  8.7 0.8 copy.90
  9.6 0.2 convert_reduce_fusion
  10.0 14.5 %all_to_all.11 = s32[16,1,3]{2,1,0:T(1,128)S(1)} all-to-all(s32[16,1,3]{2,1,0:T(1,128)S(1)} %bitcast.84), channel_id=1, replica_groups=mesh['dp'=16,'mp'=8] {'dp'}, dimensions={0} | all-to-all | bytes 384 | tf_op jit(solution)/shard_map/all_to_all | solution.py:40
  24.9 9.8 %gather_fusion = bf16[48,128,896]{2,1,0:T(8,128)(2,1)} fusion(bf16[24,128,896]{2,1,0:T(8,128)(2,1)} %param.11, s32[1024]{0:T(1024)S(1)} %pad_clamp_fusion.1), kind=kCustom, calls=%fused_computation | custom fusion | bytes 22020288 | tf_op jit(solution)/shard_map/jit(_take)/gather | solution.py:42
  34.7 10.0 %broadcast_select_fusion = bf16[16,3,128,896]{3,2,1,0:T(8,128)(2,1)} fusion(bf16[16,3,128,896]{3,2,1,0:T(8,128)(2,1)} %bitcast.73, pred[16,3]{1,0:T(8,128)(4,1)S(1)} %copy.94), kind=kLoop, calls=%fused_computation.4 | loop fusion | flops 5505024 | bytes 22020144 | tf_op jit(solution)/shard_map/jit(_take)/select_n | solution.py:42
  44.7 5.0 all-to-all-start.1
  49.7 0.7 all-gather.5.cloned.1.call-update
  50.7 191.9 %all_gather.12 = bf16[896,512]{1,0:T(8,128)(2,1)S(1)} all-gather(bf16[56,512]{1,0:T(8,128)(2,1)S(1)} %copy-done.7), channel_id=1, replica_groups=mesh['dp'=16,'mp'=8] {'dp'}, dimensions={0}, use_global_device_ids=true | all-gather | bytes 974848 | tf_op jit(solution)/shard_map/all_gather | solution.py:54
  242.7 27.2 %all_gather.14 = bf16[896,512]{1,0:T(8,128)(2,1)} all-gather(bf16[56,512]{1,0:T(8,128)(2,1)S(1)} %copy-done.8), channel_id=1, replica_groups=mesh['dp'=16,'mp'=8] {'dp'}, dimensions={0}, use_global_device_ids=true | all-gather | bytes 974848 | tf_op jit(solution)/shard_map/all_gather | solution.py:49
  269.9 3.1 multiply_reduce_fusion.1
  273.1 5.8 fusion.29
  278.9 0.1 reshape.230
  279.1 5.8 convolution_convert_fusion.8
  284.9 0.1 reshape.233
  285.1 7.0 gather_fusion.1
  292.1 4.4 broadcast_select_fusion.1
  296.5 0.9 bitcast_select_fusion
  297.4 1.8 copy-done.6
  299.3 3.8 convolution_convert_fusion.5
  303.1 2.5 reshape.229
  305.6 6.0 convolution_convert_fusion.4
  311.6 4.1 reshape.231
  315.7 2.4 fusion.15
  318.2 2.1 fusion.70
  320.3 2.2 fusion.9
  322.5 16.6 %convert_bitcast_fusion.1 = bf16[8,256,4,128]{1,3,2,0:T(8,128)(2,1)} fusion(f32[8,4,64,256]{3,2,1,0:T(8,128)} %fusion.9, bf16[8,64,4,128]{3,2,1,0:T(4,128)(2,1)S(1)} %reshape.230, f32[8,4,64,256]{3,2,1,0:T(8,128)} %get-tuple-element.11, f32[8,4,64]{2,1,0:T(4,128)S(1)} %get-tuple-element.10), kind=kOutput, calls=%fused_computation.17 | convolution fusion | flops 138938624 | bytes 6823936 | tf_op jit(solution)/shard_map/chqk,cqhd->ckhd/dot_general | solution.py:100
  339.0 2.8 copy.106
  341.8 0.7 copy.112
  342.5 1.3 copy-done.4
  343.8 3.0 convolution_convert_fusion.7
  346.9 0.3 reduce-scatter.18.cloned.1.call-start
  347.2 7.0 convert_bitcast_fusion
  354.2 2.8 copy.108
  357.0 0.7 copy.113
  357.7 1.3 copy-done.5
  359.0 3.0 convolution_convert_fusion.6
  362.1 15.3 %fusion.35 = bf16[8,64,4,128]{3,1,2,0:T(8,128)(2,1)S(1)} fusion(bf16[8,256,4,128]{3,2,1,0:T(4,128)(2,1)} %reshape.231, f32[8,4,64,256]{3,2,1,0:T(8,128)} %fusion.9, f32[8,4,64,256]{3,2,1,0:T(8,128)} %get-tuple-element.11, f32[8,4,64]{2,1,0:T(4,128)S(1)} %get-tuple-element.10), kind=kOutput, calls=%fused_computation.42 | convolution fusion | flops 138152192 | bytes 6823936 | tf_op jit(solution)/shard_map/chqk,ckhd->cqhd/dot_general | solution.py:96
  377.4 0.4 copy.104
  377.9 6.6 convolution_convert_fusion.2
  384.5 0.3 reduce-scatter.12.cloned.1.call-start
  384.8 6.6 convolution_convert_fusion.1
  391.5 5.3 fusion.32
  396.7 0.4 copy.100
  397.2 6.5 convolution_convert_fusion
  403.7 0.3 reduce-scatter.10.cloned.1.call-start
  404.1 6.6 convolution_convert_fusion.3
  410.7 6.5 convert_element_type.97
  417.2 2.3 reduce-scatter.16.cloned.1.call-done
  419.5 1.5 convert_element_type.122
  421.0 74.8 %reduce-scatter.18.cloned.1.call-done = bf16[56,512]{1,0:T(8,128)(2,1)} async-done(((bf16[896,512]{1,0:T(8,128)(2,1)}), bf16[56,512]{1,0:T(8,128)(2,1)}) %reduce-scatter.18.cloned.1.call-update) | async-done | bytes 57360
  495.8 1.5 convert_element_type.126
  497.3 72.8 %all-reduce.4.cloned.1.call-done = bf16[512,4096]{1,0:T(8,128)(2,1)} async-done(((bf16[512,4096]{1,0:T(8,128)(2,1)}), bf16[512,4096]{1,0:T(8,128)(2,1)}) %all-reduce.4.cloned.1.call-update) | async-done | bytes 4194320 | tf_op jit(solution)/shard_map/psum | solution.py:132
  570.1 3.4 convert_element_type.115
  573.6 1.3 copy-done.2
  574.8 4.6 multiply_reduce_fusion
  579.5 2.5 fusion.42
  582.0 69.7 %reduce-scatter.12.cloned.1.call-done = bf16[256,512]{1,0:T(8,128)(2,1)} async-done(((bf16[4096,512]{1,0:T(8,128)(2,1)}), bf16[256,512]{1,0:T(8,128)(2,1)}) %reduce-scatter.12.cloned.1.call-update) | async-done | bytes 262160 | tf_op jit(solution)/shard_map/reduce_scatter | solution.py:113
  651.7 1.8 convert_element_type.118
  653.5 79.3 %reduce-scatter.14.cloned.1.call-done = bf16[512,256]{1,0:T(8,128)(2,1)} async-done(((bf16[512,4096]{1,0:T(8,128)(2,1)}), bf16[512,256]{1,0:T(8,128)(2,1)}) %reduce-scatter.14.cloned.1.call-update) | async-done | bytes 262160 | tf_op jit(solution)/shard_map/reduce_scatter | solution.py:122
  732.8 1.8 convert_element_type.128
  734.6 38.1 %reduce-scatter.10.cloned.1.call-done = bf16[512,512]{1,0:T(8,128)(2,1)} async-done(((bf16[512,4096]{1,0:T(8,128)(2,1)}), bf16[512,512]{1,0:T(8,128)(2,1)}) %reduce-scatter.10.cloned.1.call-update) | async-done | bytes 524304 | tf_op jit(solution)/shard_map/reduce_scatter | solution.py:78
  772.7 2.3 add_convert_fusion
  (57 shorter events, 1.5 us)
Async XLA Ops:
  7.2 265.9 %all-gather.3.cloned.1.call-start = ((), (), s32[]{:S(2)}) async-start(), calls=%async_computation.7 | async-start | bytes 4456448 | tf_op jit(solution)/shard_map/all_gather | solution.py:28
  44.7 5.8 copy-start.9
  44.7 6.0 copy-start.7
  44.7 198.0 %copy-start.8 = (bf16[56,512]{1,0:T(8,128)(2,1)S(1)}, bf16[56,512]{1,0:T(8,128)(2,1)}, u32[]{:S(2)}) copy-start(bf16[56,512]{1,0:T(8,128)(2,1)} %param.16) | copy-start | bytes 172036
  44.7 240.4 %all-to-all-start.1 = ((bf16[16,3,128,896]{3,2,1,0:T(8,128)(2,1)}), bf16[16,3,128,896]{3,2,1,0:T(8,128)(2,1)}, u32[]{:S(2)}, u32[]{:S(2)}) async-start(bf16[16,3,128,896]{3,2,1,0:T(8,128)(2,1)} %broadcast_select_fusion), calls=%async_computation.1 | async-start | bytes 22020096 | tf_op jit(solution)/shard_map/all_to_all | solution.py:43
  49.7 229.4 %all-gather.5.cloned.1.call-start = ((), (), s32[]{:S(2)}) async-start(), calls=%async_computation.8 | async-start | bytes 4456448 | tf_op jit(solution)/shard_map/all_gather | solution.py:29
  50.4 369.0 %reduce-scatter.16.cloned.1.call-start = ((), (), s32[]{:S(2)}) async-start(), calls=%async_computation.13 | async-start | bytes 974848
  269.9 3.1 copy-start.10
  292.1 4.4 copy-start.1
  297.4 1.8 copy-start.6
  318.2 2.1 copy-start.3
  341.8 2.0 copy-start.4
  346.9 148.9 %reduce-scatter.18.cloned.1.call-start = ((), (), s32[]{:S(2)}) async-start(), calls=%async_computation.14 | async-start | bytes 974848
  357.0 2.0 copy-start.5
  362.1 208.0 %all-reduce.4.cloned.1.call-start = ((), (), s32[]{:S(2)}) async-start(), calls=%async_computation.10 | async-start | bytes 8388608 | tf_op jit(solution)/shard_map/psum | solution.py:132
  384.5 267.2 %reduce-scatter.12.cloned.1.call-start = ((), (), s32[]{:S(2)}) async-start(), calls=%async_computation.11 | async-start | bytes 4456448 | tf_op jit(solution)/shard_map/reduce_scatter | solution.py:113
  391.4 341.3 %reduce-scatter.14.cloned.1.call-start = ((), (), s32[]{:S(2)}) async-start(), calls=%async_computation.12 | async-start | bytes 4456448 | tf_op jit(solution)/shard_map/reduce_scatter | solution.py:122
  403.7 368.9 %reduce-scatter.10.cloned.1.call-start = ((), (), s32[]{:S(2)}) async-start(), calls=%async_computation.9 | async-start | bytes 4718592 | tf_op jit(solution)/shard_map/reduce_scatter | solution.py:78
  570.1 3.4 copy-start
  570.1 4.7 copy-start.2
Sparse Core Ops, SparseCore 0:
  10.1 158.5 all-gather.2
  170.8 90.4 all-gather.4
  347.0 72.4 reduce-scatter.15
  422.5 73.2 reduce-scatter.17
  498.0 72.0 all-reduce.3
  573.3 78.3 reduce-scatter.11
  655.0 77.7 reduce-scatter.13
  735.2 37.4 reduce-scatter.9
where the time goes:
time: 787 us; the launch traced here: 782 us
  waiting for transfers between devices  339 us (43%)
  blocking collectives  234 us (30%)
  matrix products  103 us (13%)
  other arithmetic  47.6 us (6%)
  local copies, waits for them, and re-layouts  39 us (5%)
  between operations  14.9 us (2%)
    all_gather x1, blocking collectives, on_device(): lax.all_gather(w_value, 'dp', axis=0, tiled=True)  192 us
    reduce_scatter x1, waiting for transfers between devices, on_device(): lax.psum_scatter(grad_wout_part.astype(jnp.bfloat16), 'dp', scatter_dimen...  79.3 us
    unnamed x10, waiting for transfers between devices  78.6 us
    psum x1, waiting for transfers between devices, on_device(): lax.psum(grad_normed_part.astype(jnp.bfloat16), 'mp').astype(jnp.float32)  72.8 us
    reduce_scatter x1, waiting for transfers between devices, on_device(): lax.psum_scatter(grad_wq_part.astype(jnp.bfloat16), 'dp', scatter_dimensi...  69.7 us
    reduce_scatter x1, waiting for transfers between devices, on_device(): lax.psum_scatter(partial_out.astype(jnp.bfloat16), 'mp', scatter_dimensio...  38.1 us
    all_gather x1, blocking collectives, on_device(): lax.all_gather(w_key, 'dp', axis=0, tiled=True)  27.2 us
    dot_general x1, matrix products, on_device(): jnp.einsum('chqk,cqhd->ckhd', grad_scores, query_blocks, preferred_elemen...  16.6 us
  transfers between devices with their start and end apart: 9, of which 6 were waited for; matrix products, arithmetic and copies ran while one was open for 16% of the time, Pallas kernels for 0%

commit v1 on v0

--- a/solution.py
+++ b/solution.py
@@ -1,12 +1,21 @@
+import functools
 import jax
 import jax.numpy as jnp
 from jax import lax
 from jax.sharding import PartitionSpec as P
+from jax.lax import all_gather
 
 HD = 128
 CL = 64
 KN = 2
 CAP = 3
+
+
+def meet_the_field(local, shard_axis):
+    return jnp.sum(all_gather(local, axis_name=shard_axis), 0)
+
+
+drive_roots = functools.partial(meet_the_field, shard_axis="mp")
 
 
 def on_device(tokens, cache, nb_row, nb_owner, nb_len, w_query, w_key, w_value, w_out, grad_out):
@@ -129,7 +138,7 @@
     out_cols = lax.dynamic_slice_in_dim(grad_out, mp_place * width_share, width_share, 1).astype(
         jnp.float32
     )
-    grad_normed = lax.psum(grad_normed_part.astype(jnp.bfloat16), "mp").astype(jnp.float32)
+    grad_normed = drive_roots(grad_normed_part.astype(jnp.bfloat16)).astype(jnp.float32)
     stat_rows = jnp.mean(grad_normed * normed_wide, axis=1, keepdims=True)
     grad_full = inv_rms * (grad_normed - normed_wide * stat_rows)
     grad_here = lax.dynamic_slice_in_dim(grad_full, mp_place * width_share, width_share, 1)

time: 787 us -> 884 us (1.12)
  waiting for transfers between devices: 339 us -> 429 us
  other arithmetic: 47.6 us -> 61.4 us
    all_gather x1, blocking collectives: 192 us -> 27.2 us  [on_device(): lax.all_gather(w_value, 'dp', axis=0, tiled=True)]
    all_gather x1, blocking collectives: 27.2 us -> 192 us  [on_device(): lax.all_gather(w_key, 'dp', axis=0, tiled=True)]
    all_gather x0 -> x1, waiting for transfers between devices: none -> 154 us  [meet_the_field(): return jnp.sum(all_gather(local, axis_name=shard_axis), 0)]
    psum x1 -> x0, waiting for transfers between devices: 72.8 us -> none  [on_device(): lax.psum(grad_normed_part.astype(jnp.bfloat16), 'mp').astype(jnp.float32)]
    reduce_sum x0 -> x1, other arithmetic: none -> 14.2 us  [meet_the_field(): return jnp.sum(all_gather(local, axis_name=shard_axis), 0)]
    reduce_scatter x1, waiting for transfers between devices: 69.7 us -> 79.2 us  [on_device(): lax.psum_scatter(grad_wq_part.astype(jnp.bfloat16), 'dp', scatter_dimensi...]
  transfers between devices with their start and end apart: 9 -> 9, of which waited for: 6 -> 6; matrix products, arithmetic and copies ran while one was open for 16% -> 13% of each run, Pallas kernels for 0% -> 0%
where the time goes in v1:
time: 884 us; the launch traced here: 879 us
  waiting for transfers between devices  429 us (49%)
  blocking collectives  234 us (26%)
  matrix products  97.3 us (11%)
  other arithmetic  61.4 us (7%)
  local copies, waits for them, and re-layouts  36.1 us (4%)
  between operations  14.9 us (2%)
    all_gather x1, blocking collectives, on_device(): lax.all_gather(w_key, 'dp', axis=0, tiled=True)  192 us
    all_gather x1, waiting for transfers between devices, meet_the_field(): return jnp.sum(all_gather(local, axis_name=shard_axis), 0)  154 us
    reduce_scatter x1, waiting for transfers between devices, on_device(): lax.psum_scatter(grad_wout_part.astype(jnp.bfloat16), 'dp', scatter_dimen...  79.5 us
    reduce_scatter x1, waiting for transfers between devices, on_device(): lax.psum_scatter(grad_wq_part.astype(jnp.bfloat16), 'dp', scatter_dimensi...  79.2 us
    unnamed x10, waiting for transfers between devices  78.6 us
    reduce_scatter x1, waiting for transfers between devices, on_device(): lax.psum_scatter(partial_out.astype(jnp.bfloat16), 'mp', scatter_dimensio...  38 us
    all_gather x1, blocking collectives, on_device(): lax.all_gather(w_value, 'dp', axis=0, tiled=True)  27.2 us
  transfers between devices with their start and end apart: 9, of which 6 were waited for; matrix products, arithmetic and copies ran while one was open for 13% of the time, Pallas kernels for 0%

profile of v1, /device:TPU:0, one launch (start us, length us, event | category | flops | bytes accessed | tf_op | source)
XLA Modules:
  0.0 878.7 jit_solution(9485151459332659931)
XLA Ops:
  7.2 0.7 all-gather.5.cloned.1.call-update
  7.9 0.7 broadcast_add_fusion
  8.7 0.8 copy.90
  9.6 0.2 convert_reduce_fusion
  10.0 14.5 %all_to_all.11 = s32[16,1,3]{2,1,0:T(1,128)S(1)} all-to-all(s32[16,1,3]{2,1,0:T(1,128)S(1)} %bitcast.86), channel_id=1, replica_groups=mesh['dp'=16,'mp'=8] {'dp'}, dimensions={0} | all-to-all | bytes 384 | tf_op jit(solution)/shard_map/all_to_all | solution.py:49
  24.9 9.8 %gather_fusion = bf16[48,128,896]{2,1,0:T(8,128)(2,1)} fusion(bf16[24,128,896]{2,1,0:T(8,128)(2,1)} %param.11, s32[1024]{0:T(1024)S(1)} %pad_clamp_fusion.1), kind=kCustom, calls=%fused_computation | custom fusion | bytes 22020288 | tf_op jit(solution)/shard_map/jit(_take)/gather | solution.py:51
  34.7 10.0 %broadcast_select_fusion = bf16[16,3,128,896]{3,2,1,0:T(8,128)(2,1)} fusion(bf16[16,3,128,896]{3,2,1,0:T(8,128)(2,1)} %bitcast.74, pred[16,3]{1,0:T(8,128)(4,1)S(1)} %copy.94), kind=kLoop, calls=%fused_computation.4 | loop fusion | flops 5505024 | bytes 22020144 | tf_op jit(solution)/shard_map/jit(_take)/select_n | solution.py:51
  44.7 5.0 all-to-all-start.1
  49.7 0.7 all-gather.7.cloned.1.call-update
  50.7 191.9 %all_gather.20 = bf16[896,512]{1,0:T(8,128)(2,1)S(1)} all-gather(bf16[56,512]{1,0:T(8,128)(2,1)S(1)} %copy-done.8), channel_id=1, replica_groups=mesh['dp'=16,'mp'=8] {'dp'}, dimensions={0}, use_global_device_ids=true | all-gather | bytes 974848 | tf_op jit(solution)/shard_map/all_gather | solution.py:58
  242.6 27.2 %all_gather.18 = bf16[896,512]{1,0:T(8,128)(2,1)} all-gather(bf16[56,512]{1,0:T(8,128)(2,1)S(1)} %copy-done.9), channel_id=1, replica_groups=mesh['dp'=16,'mp'=8] {'dp'}, dimensions={0}, use_global_device_ids=true | all-gather | bytes 974848 | tf_op jit(solution)/shard_map/all_gather | solution.py:63
  269.9 3.1 multiply_reduce_fusion.1
  273.1 5.8 fusion.29
  278.9 0.1 reshape.230
  279.1 5.8 convolution_convert_fusion.8
  285.0 7.0 gather_fusion.1
  292.1 4.4 broadcast_select_fusion.1
  296.5 0.9 bitcast_select_fusion
  297.4 3.7 convolution_convert_fusion.4
  301.1 2.4 convolution_convert_fusion.5
  303.5 2.1 reshape.229
  305.6 2.7 reshape.231
  308.4 0.8 fusion.15
  309.2 0.7 copy-done.3
  310.0 2.1 fusion.9
  312.1 1.8 fusion.70
  313.9 16.6 %convert_bitcast_fusion.1 = bf16[8,256,4,128]{1,3,2,0:T(8,128)(2,1)} fusion(f32[8,4,64,256]{3,2,1,0:T(8,128)} %fusion.9, bf16[8,64,4,128]{3,2,1,0:T(4,128)(2,1)S(1)} %reshape.230, f32[8,4,64,256]{3,2,1,0:T(8,128)} %get-tuple-element.11, f32[8,4,64]{2,1,0:T(4,128)S(1)} %get-tuple-element.10), kind=kOutput, calls=%fused_computation.17 | convolution fusion | flops 138938624 | bytes 6823936 | tf_op jit(solution)/shard_map/chqk,cqhd->ckhd/dot_general | solution.py:109
  330.5 2.8 copy.106
  333.3 0.7 copy.112
  334.0 1.3 copy-done.5
  335.3 3.1 convolution_convert_fusion.7
  338.4 0.3 reduce-scatter.18.cloned.1.call-start
  338.6 7.0 convert_bitcast_fusion
  345.7 2.8 copy.108
  348.5 0.7 copy.113
  349.2 1.3 copy-done.6
  350.5 3.1 convolution_convert_fusion.6
  353.6 5.9 fusion.32
  359.5 0.4 copy.100
  359.9 6.5 convolution_convert_fusion
  366.4 0.3 reduce-scatter.12.cloned.1.call-start
  366.7 14.7 %fusion.35 = bf16[8,64,4,128]{3,1,2,0:T(8,128)(2,1)S(1)} fusion(bf16[8,256,4,128]{3,2,1,0:T(4,128)(2,1)S(1)} %reshape.231, f32[8,4,64,256]{3,2,1,0:T(8,128)} %fusion.9, f32[8,4,64,256]{3,2,1,0:T(8,128)} %get-tuple-element.11, f32[8,4,64]{2,1,0:T(4,128)S(1)} %get-tuple-element.10), kind=kOutput, calls=%fused_computation.42 | convolution fusion | flops 138152192 | bytes 6823936 | tf_op jit(solution)/shard_map/chqk,ckhd->cqhd/dot_general | solution.py:105
  381.5 0.4 copy.104
  381.9 6.6 convolution_convert_fusion.1
  388.6 6.5 convolution_convert_fusion.3
  395.1 0.3 all-gather.9.cloned.1.call-start
  395.5 6.6 convolution_convert_fusion.2
  402.1 6.5 convert_element_type.99
  408.6 2.3 reduce-scatter.16.cloned.1.call-done
  410.9 1.5 convert_element_type.124
  412.4 74.9 %reduce-scatter.18.cloned.1.call-done = bf16[56,512]{1,0:T(8,128)(2,1)} async-done(((bf16[896,512]{1,0:T(8,128)(2,1)}), bf16[56,512]{1,0:T(8,128)(2,1)}) %reduce-scatter.18.cloned.1.call-update) | async-done | bytes 57360
  487.2 1.5 convert_element_type.128
  488.7 79.5 %reduce-scatter.14.cloned.1.call-done = bf16[512,256]{1,0:T(8,128)(2,1)} async-done(((bf16[512,4096]{1,0:T(8,128)(2,1)}), bf16[512,256]{1,0:T(8,128)(2,1)}) %reduce-scatter.14.cloned.1.call-update) | async-done | bytes 262160 | tf_op jit(solution)/shard_map/reduce_scatter | solution.py:131
  568.2 1.8 convert_element_type.130
  570.0 79.2 %reduce-scatter.12.cloned.1.call-done = bf16[256,512]{1,0:T(8,128)(2,1)} async-done(((bf16[4096,512]{1,0:T(8,128)(2,1)}), bf16[256,512]{1,0:T(8,128)(2,1)}) %reduce-scatter.12.cloned.1.call-update) | async-done | bytes 262160 | tf_op jit(solution)/shard_map/reduce_scatter | solution.py:122
  649.1 1.8 convert_element_type.120
  650.9 38.0 %reduce-scatter.10.cloned.1.call-done = bf16[512,512]{1,0:T(8,128)(2,1)} async-done(((bf16[512,4096]{1,0:T(8,128)(2,1)}), bf16[512,512]{1,0:T(8,128)(2,1)}) %reduce-scatter.10.cloned.1.call-update) | async-done | bytes 524304 | tf_op jit(solution)/shard_map/reduce_scatter | solution.py:87
  689.0 2.3 add_convert_fusion
  691.3 154.0 %all-gather.9.cloned.1.call-done = bf16[4096,4096]{1,0:T(8,128)(2,1)} async-done(((bf16[512,4096]{1,0:T(8,128)(2,1)}), bf16[4096,4096]{1,0:T(8,128)(2,1)}) %all-gather.9.cloned.1.call-update) | async-done | bytes 33554448 | tf_op jit(solution)/shard_map/all_gather | solution.py:15
  845.4 14.2 %reduce_sum.74 = bf16[512,4096]{1,0:T(8,128)(2,1)} reduce(bf16[8,512,4096]{2,1,0:T(8,128)(2,1)} %bitcast.75, bf16[]{:T(256)} %constant.63.clone.1), dimensions={0}, to_apply=%region_7.8 | reduce | flops 14680064 | bytes 37748736 | tf_op jit(solution)/shard_map/reduce_sum | solution.py:15
  859.5 3.4 convert_element_type.117
  863.0 1.3 copy-done.1
  864.2 4.6 multiply_reduce_fusion
  868.9 2.5 fusion.42
  (60 shorter events, 1.7 us)
Async XLA Ops:
  7.2 265.9 %all-gather.5.cloned.1.call-start = ((), (), s32[]{:S(2)}) async-start(), calls=%async_computation.7 | async-start | bytes 4456448 | tf_op jit(solution)/shard_map/all_gather | solution.py:37
  44.7 5.8 copy-start.10
  44.7 6.0 copy-start.8
  44.7 197.9 %copy-start.9 = (bf16[56,512]{1,0:T(8,128)(2,1)S(1)}, bf16[56,512]{1,0:T(8,128)(2,1)}, u32[]{:S(2)}) copy-start(bf16[56,512]{1,0:T(8,128)(2,1)} %param.17) | copy-start | bytes 172036
  44.7 240.4 %all-to-all-start.1 = ((bf16[16,3,128,896]{3,2,1,0:T(8,128)(2,1)}), bf16[16,3,128,896]{3,2,1,0:T(8,128)(2,1)}, u32[]{:S(2)}, u32[]{:S(2)}) async-start(bf16[16,3,128,896]{3,2,1,0:T(8,128)(2,1)} %broadcast_select_fusion), calls=%async_computation.1 | async-start | bytes 22020096 | tf_op jit(solution)/shard_map/all_to_all | solution.py:52
  49.7 229.4 %all-gather.7.cloned.1.call-start = ((), (), s32[]{:S(2)}) async-start(), calls=%async_computation.8 | async-start | bytes 4456448 | tf_op jit(solution)/shard_map/all_gather | solution.py:38
  50.4 360.5 %reduce-scatter.16.cloned.1.call-start = ((), (), s32[]{:S(2)}) async-start(), calls=%async_computation.13 | async-start | bytes 974848
  269.9 3.1 copy-start.11
  292.1 4.4 copy-start.2
  297.4 3.7 copy-start.7
  308.4 1.6 copy-start.3
  310.0 2.2 copy-start.4
  333.3 2.0 copy-start.5
  338.4 148.8 %reduce-scatter.18.cloned.1.call-start = ((), (), s32[]{:S(2)}) async-start(), calls=%async_computation.14 | async-start | bytes 974848
  348.5 2.0 copy-start.6
  353.6 214.6 %reduce-scatter.14.cloned.1.call-start = ((), (), s32[]{:S(2)}) async-start(), calls=%async_computation.11 | async-start | bytes 4456448 | tf_op jit(solution)/shard_map/reduce_scatter | solution.py:131
  366.4 282.7 %reduce-scatter.12.cloned.1.call-start = ((), (), s32[]{:S(2)}) async-start(), calls=%async_computation.10 | async-start | bytes 4456448 | tf_op jit(solution)/shard_map/reduce_scatter | solution.py:122
  388.6 300.4 %reduce-scatter.10.cloned.1.call-start = ((), (), s32[]{:S(2)}) async-start(), calls=%async_computation.9 | async-start | bytes 4718592 | tf_op jit(solution)/shard_map/reduce_scatter | solution.py:87
  395.1 450.2 %all-gather.9.cloned.1.call-start = ((), (), s32[]{:S(2)}) async-start(), calls=%async_computation.12 | async-start | bytes 37748736 | tf_op jit(solution)/shard_map/all_gather | solution.py:15
  859.5 3.4 copy-start
  859.5 4.7 copy-start.1
Sparse Core Ops, SparseCore 0:
  10.1 158.5 all-gather.4
  170.8 90.3 all-gather.6
  338.5 72.3 reduce-scatter.15
  414.0 73.2 reduce-scatter.17
  490.4 77.7 reduce-scatter.13
  571.4 77.7 reduce-scatter.11
  651.5 37.4 reduce-scatter.9
  690.7 154.6 all-gather.8
